TPU v7x, 32 devices: a whole 2x2x4 slice. The times are simulated.
32 devices in a mesh: dp: 8 (over z, y), tensor: 4 (over x, core).
Axes of the slice: x: 2, y: 2, z: 4, core: 2. Of those that a mesh axis runs over, the one named last changes fastest.
Arguments:
- inputs: bfloat16 [8192, 1536], P('dp', 'tensor'), may hold values from -6 to 6
- segment_ids: int32 [8192], P('dp'), may hold values from 0 to 26, never falling along the last dimension, each value on 1 to 1000 neighbouring positions
- cotangent: bfloat16 [8192, 1536], P('dp', 'tensor'), may hold values from -6 to 6
- first_gain: bfloat16 [1536], replicated, may hold values from 0.5 to 1.5
- gate_weight: bfloat16 [1536, 2048], P(None, 'tensor'), may hold values from -0.15625 to 0.15625
- gate_bias: bfloat16 [2048], P('tensor'), may hold values from -3 to 3
- branch_weight: bfloat16 [1536, 2048], P(None, 'tensor'), may hold values from -0.15625 to 0.15625
- branch_bias: bfloat16 [2048], P('tensor'), may hold values from -3 to 3
- conv_weight: bfloat16 [4, 2048], P(None, 'tensor'), may hold values from -3 to 3
- conv_bias: bfloat16 [2048], P('tensor'), may hold values from -3 to 3
- rate_weight: bfloat16 [16, 128, 128], P('tensor'), may hold values from -0.5 to 0.5
- rate_bias: bfloat16 [2048], P('tensor'), may hold values from -3 to 3
- input_weight: bfloat16 [16, 128, 128], P('tensor'), may hold values from -0.5 to 0.5
- input_bias: bfloat16 [2048], P('tensor'), may hold values from -3 to 3
- decay_param: float32 [2048], P('tensor'), may hold values from 3 to 7
- out_weight: bfloat16 [2048, 1536], P('tensor'), may hold values from -0.25 to 0.25
- second_gain: bfloat16 [1536], replicated, may hold values from 0.5 to 1.5
- ffn_gate: bfloat16 [1536, 4608], P(None, 'tensor'), may hold values from -0.15625 to 0.15625
- ffn_up: bfloat16 [1536, 4608], P(None, 'tensor'), may hold values from -0.15625 to 0.15625
- ffn_down: bfloat16 [4608, 1536], P('tensor'), may hold values from -0.1875 to 0.1875
Outputs:
- output: bfloat16 [8192, 1536], P('dp', 'tensor')
- input_grad: float32 [8192, 1536], P('dp', 'tensor')
- first_gain_grad: float32 [1536], replicated
- gate_weight_grad: float32 [1536, 2048], P(None, 'tensor')
- gate_bias_grad: float32 [2048], P('tensor')
- branch_weight_grad: float32 [1536, 2048], P(None, 'tensor')
- branch_bias_grad: float32 [2048], P('tensor')
- conv_weight_grad: float32 [4, 2048], P(None, 'tensor')
- conv_bias_grad: float32 [2048], P('tensor')
- rate_weight_grad: float32 [16, 128, 128], P('tensor')
- rate_bias_grad: float32 [2048], P('tensor')
- input_weight_grad: float32 [16, 128, 128], P('tensor')
- input_bias_grad: float32 [2048], P('tensor')
- decay_grad: float32 [2048], P('tensor')
- out_weight_grad: float32 [2048, 1536], P('tensor')
- second_gain_grad: float32 [1536], replicated
- ffn_gate_grad: float32 [1536, 4608], P(None, 'tensor')
- ffn_up_grad: float32 [1536, 4608], P(None, 'tensor')
- ffn_down_grad: float32 [4608, 1536], P('tensor')
Inputs may be any that keep to these rules, and one draw needn't show every extreme that they name: `segment_ids`: segment numbers never fall along the tokens; each document has 1 to 1000 consecutive tokens, one exactly 1000.
All inputs are finite; a program needn't handle non-finite values.
Results may differ from a plain program's by a relative error of at most 0.013.
Values may be sent and summed in bfloat16 or wider, within the bound.
A program may use at most 256 MiB of HBM per device.

v0:
```python
import jax
import jax.numpy as jnp
from jax import lax
from jax.sharding import PartitionSpec as P

SEQ = 1024
EPSILON = 1e-06
FLOOR = 0.05


def rms_scale(values, gain):
    return values * lax.rsqrt(jnp.mean(values * values, axis=-1, keepdims=True) + EPSILON) * gain


def seq_masks(segments, length):
    count = segments.shape[0]
    place = jnp.arange(count, dtype=jnp.int32) % length
    previous = jnp.concatenate([segments[:1], segments[:-1]])
    reset = (place == 0) | (segments != previous)
    return (place, reset)


def conv_apply(values, weights, shift_bias, segments, place):
    total = shift_bias + weights[0] * values
    for offset in range(1, weights.shape[0]):
        moved = jnp.concatenate(
            [jnp.zeros((offset, values.shape[1]), values.dtype), values[:-offset]]
        )
        earlier = jnp.concatenate([jnp.full((offset,), -1, jnp.int32), segments[:-offset]])
        usable = ((place >= offset) & (segments == earlier)).astype(values.dtype)
        total = total + weights[offset] * moved * usable[:, None]
    return total


def gates_to_step(rate_pre, input_pre, conv_out, decay, reset):
    rate = jax.nn.sigmoid(rate_pre)
    opened = jax.nn.sigmoid(input_pre)
    decayed = jnp.exp(-8.0 * rate * jax.nn.softplus(-decay))
    keep = jnp.where(reset[:, None], jnp.zeros_like(decayed), decayed)
    scale = jnp.where(
        reset[:, None],
        jnp.ones_like(decayed),
        jnp.sqrt(jnp.maximum(1.0 - decayed * decayed, FLOOR)),
    )
    return (keep, scale * opened * conv_out)


def combine(earlier, later):
    return (earlier[0] * later[0], later[0] * earlier[1] + later[1])


def block_mix(values, weight):
    rows = values.shape[0]
    split = values.reshape(rows, weight.shape[0], -1)
    return jnp.einsum("thi,hij->thj", split, weight, preferred_element_type=jnp.float32).reshape(
        rows, -1
    )


def block_back(grads, weight):
    rows = grads.shape[0]
    split = grads.reshape(rows, weight.shape[0], -1)
    return jnp.einsum("thj,hij->thi", split, weight, preferred_element_type=jnp.float32).reshape(
        rows, -1
    )


def block_grad(values, grads, heads):
    rows = values.shape[0]
    left = values.reshape(rows, heads, -1)
    right = grads.reshape(rows, heads, -1)
    return jnp.einsum("thi,thj->hij", left, right, preferred_element_type=jnp.float32)


def column_sum(values):
    return jnp.sum(values.astype(jnp.float32), axis=0)


def body(
    inputs,
    segment_ids,
    cotangent,
    first_gain,
    gate_weight,
    gate_bias,
    branch_weight,
    branch_bias,
    conv_weight,
    conv_bias,
    rate_weight,
    rate_bias,
    input_weight,
    input_bias,
    decay_param,
    out_weight,
    second_gain,
    ffn_gate,
    ffn_up,
    ffn_down,
):
    share = inputs.shape[1]
    heads = rate_weight.shape[0]
    offset = lax.axis_index("tensor") * share
    place, reset = seq_masks(segment_ids, SEQ)
    whole_in = lax.all_gather(inputs, "tensor", axis=1, tiled=True).astype(jnp.float32)
    normed_one, first_pull = jax.vjp(rms_scale, whole_in, first_gain.astype(jnp.float32))
    normed_low = normed_one.astype(jnp.bfloat16)
    gate_pre = jnp.dot(
        normed_low, gate_weight, preferred_element_type=jnp.float32
    ) + gate_bias.astype(jnp.float32)
    branch_pre = jnp.dot(
        normed_low, branch_weight, preferred_element_type=jnp.float32
    ) + branch_bias.astype(jnp.float32)

    def conv_local(values, weights, shift_bias):
        return conv_apply(values, weights, shift_bias, segment_ids, place)

    conv_out, conv_pull = jax.vjp(
        conv_local, branch_pre, conv_weight.astype(jnp.float32), conv_bias.astype(jnp.float32)
    )
    conv_low = conv_out.astype(jnp.bfloat16)
    rate_pre = block_mix(conv_low, rate_weight) + rate_bias.astype(jnp.float32)
    input_pre = block_mix(conv_low, input_weight) + input_bias.astype(jnp.float32)

    def step_local(rate_in, input_in, driven, decay):
        return gates_to_step(rate_in, input_in, driven, decay, reset)

    (keep, drive), step_pull = jax.vjp(step_local, rate_pre, input_pre, conv_out, decay_param)
    state = lax.associative_scan(combine, (keep, drive))[1]
    gate_act, gelu_pull = jax.vjp(jax.nn.gelu, gate_pre)
    mixed_low = (gate_act * state).astype(jnp.bfloat16)
    partial_value = jnp.dot(mixed_low, out_weight, preferred_element_type=jnp.float32)
    resid = whole_in + lax.psum(partial_value, "tensor")
    resid_mine = lax.dynamic_slice_in_dim(resid, offset, share, 1)
    normed_two, second_pull = jax.vjp(rms_scale, resid, second_gain.astype(jnp.float32))
    two_low = normed_two.astype(jnp.bfloat16)
    hidden_gate = jnp.dot(two_low, ffn_gate, preferred_element_type=jnp.float32)
    hidden_up = jnp.dot(two_low, ffn_up, preferred_element_type=jnp.float32)
    hidden_act, hidden_pull = jax.vjp(jax.nn.gelu, hidden_gate)
    hidden_low = (hidden_act * hidden_up).astype(jnp.bfloat16)
    ffn_part = jnp.dot(hidden_low, ffn_down, preferred_element_type=jnp.float32)
    output = (
        resid_mine
        + lax.psum_scatter(
            ffn_part.astype(jnp.bfloat16), "tensor", scatter_dimension=1, tiled=True
        ).astype(jnp.float32)
    ).astype(jnp.bfloat16)
    whole_cot = lax.all_gather(cotangent, "tensor", axis=1, tiled=True)
    d_hidden = jnp.einsum("td,fd->tf", whole_cot, ffn_down, preferred_element_type=jnp.float32)
    ffn_down_grad = jnp.einsum(
        "tf,td->fd", hidden_low, whole_cot, preferred_element_type=jnp.float32
    )
    d_hgate = hidden_pull(d_hidden * hidden_up)[0].astype(jnp.bfloat16)
    d_hup = (d_hidden * hidden_act).astype(jnp.bfloat16)
    ffn_gate_grad = jnp.einsum("td,tf->df", two_low, d_hgate, preferred_element_type=jnp.float32)
    ffn_up_grad = jnp.einsum("td,tf->df", two_low, d_hup, preferred_element_type=jnp.float32)
    d_two_part = jnp.einsum(
        "tf,df->td", d_hgate, ffn_gate, preferred_element_type=jnp.float32
    ) + jnp.einsum("tf,df->td", d_hup, ffn_up, preferred_element_type=jnp.float32)
    d_two = lax.psum(d_two_part, "tensor")
    d_resid_norm, second_gain_grad = second_pull(d_two)
    d_resid = whole_cot.astype(jnp.float32) + d_resid_norm
    d_resid_low = d_resid.astype(jnp.bfloat16)
    out_weight_grad = jnp.einsum(
        "tr,td->rd", mixed_low, d_resid_low, preferred_element_type=jnp.float32
    )
    d_mixed = jnp.einsum("td,rd->tr", d_resid_low, out_weight, preferred_element_type=jnp.float32)
    d_gate_low = gelu_pull(d_mixed * state)[0].astype(jnp.bfloat16)
    d_state = d_mixed * gate_act
    channels = keep.shape[1]
    keep_next = jnp.concatenate([keep[1:], jnp.zeros((1, channels), jnp.float32)])
    adjoint = lax.associative_scan(combine, (keep_next, d_state), reverse=True)[1]
    state_prev = jnp.concatenate([jnp.zeros((1, channels), jnp.float32), state[:-1]])
    d_rate, d_input, d_conv_direct, decay_grad = step_pull((adjoint * state_prev, adjoint))
    d_rate_low = d_rate.astype(jnp.bfloat16)
    d_input_low = d_input.astype(jnp.bfloat16)
    rate_weight_grad = block_grad(conv_low, d_rate_low, heads)
    input_weight_grad = block_grad(conv_low, d_input_low, heads)
    rate_bias_grad = column_sum(d_rate_low)
    input_bias_grad = column_sum(d_input_low)
    d_conv = (
        d_conv_direct + block_back(d_rate_low, rate_weight) + block_back(d_input_low, input_weight)
    )
    d_branch, conv_weight_grad, conv_bias_grad = conv_pull(d_conv)
    d_branch_low = d_branch.astype(jnp.bfloat16)
    gate_weight_grad = jnp.einsum(
        "td,tr->dr", normed_low, d_gate_low, preferred_element_type=jnp.float32
    )
    branch_weight_grad = jnp.einsum(
        "td,tr->dr", normed_low, d_branch_low, preferred_element_type=jnp.float32
    )
    gate_bias_grad = column_sum(d_gate_low)
    branch_bias_grad = column_sum(d_branch_low)
    d_first_part = jnp.einsum(
        "tr,dr->td", d_gate_low, gate_weight, preferred_element_type=jnp.float32
    ) + jnp.einsum("tr,dr->td", d_branch_low, branch_weight, preferred_element_type=jnp.float32)
    d_first = lax.psum(d_first_part.astype(jnp.bfloat16), "tensor").astype(jnp.float32)
    d_in_norm, first_gain_grad = first_pull(d_first)
    input_grad = lax.dynamic_slice_in_dim(d_resid + d_in_norm, offset, share, 1)
    pieces = (
        lax.psum_scatter(first_gain_grad, "dp", scatter_dimension=0, tiled=True),
        lax.psum_scatter(gate_weight_grad, "dp", scatter_dimension=0, tiled=True),
        lax.psum_scatter(gate_bias_grad, "dp", scatter_dimension=0, tiled=True),
        lax.psum_scatter(branch_weight_grad, "dp", scatter_dimension=0, tiled=True),
        lax.psum_scatter(branch_bias_grad, "dp", scatter_dimension=0, tiled=True),
        lax.psum_scatter(conv_weight_grad, "dp", scatter_dimension=1, tiled=True),
        lax.psum_scatter(conv_bias_grad, "dp", scatter_dimension=0, tiled=True),
        lax.psum_scatter(rate_weight_grad, "dp", scatter_dimension=1, tiled=True),
        lax.psum_scatter(rate_bias_grad, "dp", scatter_dimension=0, tiled=True),
        lax.psum_scatter(input_weight_grad, "dp", scatter_dimension=1, tiled=True),
        lax.psum_scatter(input_bias_grad, "dp", scatter_dimension=0, tiled=True),
        lax.psum_scatter(decay_grad, "dp", scatter_dimension=0, tiled=True),
        lax.psum_scatter(out_weight_grad, "dp", scatter_dimension=0, tiled=True),
        lax.psum_scatter(second_gain_grad, "dp", scatter_dimension=0, tiled=True),
        lax.psum_scatter(ffn_gate_grad, "dp", scatter_dimension=0, tiled=True),
        lax.psum_scatter(ffn_up_grad, "dp", scatter_dimension=0, tiled=True),
        lax.psum_scatter(ffn_down_grad, "dp", scatter_dimension=1, tiled=True),
    )
    done = (
        lax.all_gather(pieces[0].astype(jnp.bfloat16), "dp", axis=0, tiled=True).astype(
            jnp.float32
        ),
        lax.all_gather(pieces[1].astype(jnp.bfloat16), "dp", axis=0, tiled=True).astype(
            jnp.float32
        ),
        lax.all_gather(pieces[2].astype(jnp.bfloat16), "dp", axis=0, tiled=True).astype(
            jnp.float32
        ),
        lax.all_gather(pieces[3].astype(jnp.bfloat16), "dp", axis=0, tiled=True).astype(
            jnp.float32
        ),
        lax.all_gather(pieces[4].astype(jnp.bfloat16), "dp", axis=0, tiled=True).astype(
            jnp.float32
        ),
        lax.all_gather(pieces[5].astype(jnp.bfloat16), "dp", axis=1, tiled=True).astype(
            jnp.float32
        ),
        lax.all_gather(pieces[6].astype(jnp.bfloat16), "dp", axis=0, tiled=True).astype(
            jnp.float32
        ),
        lax.all_gather(pieces[7].astype(jnp.bfloat16), "dp", axis=1, tiled=True).astype(
            jnp.float32
        ),
        lax.all_gather(pieces[8].astype(jnp.bfloat16), "dp", axis=0, tiled=True).astype(
            jnp.float32
        ),
        lax.all_gather(pieces[9].astype(jnp.bfloat16), "dp", axis=1, tiled=True).astype(
            jnp.float32
        ),
        lax.all_gather(pieces[10].astype(jnp.bfloat16), "dp", axis=0, tiled=True).astype(
            jnp.float32
        ),
        lax.all_gather(pieces[11].astype(jnp.bfloat16), "dp", axis=0, tiled=True).astype(
            jnp.float32
        ),
        lax.all_gather(pieces[12].astype(jnp.bfloat16), "dp", axis=0, tiled=True).astype(
            jnp.float32
        ),
        lax.all_gather(pieces[13].astype(jnp.bfloat16), "dp", axis=0, tiled=True).astype(
            jnp.float32
        ),
        lax.all_gather(pieces[14].astype(jnp.bfloat16), "dp", axis=0, tiled=True).astype(
            jnp.float32
        ),
        lax.all_gather(pieces[15].astype(jnp.bfloat16), "dp", axis=0, tiled=True).astype(
            jnp.float32
        ),
        lax.all_gather(pieces[16].astype(jnp.bfloat16), "dp", axis=1, tiled=True).astype(
            jnp.float32
        ),
    )
    return (
        output,
        input_grad,
        done[0],
        done[1],
        done[2],
        done[3],
        done[4],
        done[5],
        done[6],
        done[7],
        done[8],
        done[9],
        done[10],
        done[11],
        done[12],
        done[13],
        done[14],
        done[15],
        done[16],
    )


def solution(mesh):
    in_specs = (
        P("dp", "tensor"),
        P("dp"),
        P("dp", "tensor"),
        P(),
        P(None, "tensor"),
        P("tensor"),
        P(None, "tensor"),
        P("tensor"),
        P(None, "tensor"),
        P("tensor"),
        P("tensor", None, None),
        P("tensor"),
        P("tensor", None, None),
        P("tensor"),
        P("tensor"),
        P("tensor", None),
        P(),
        P(None, "tensor"),
        P(None, "tensor"),
        P("tensor", None),
    )
    out_specs = (
        P("dp", "tensor"),
        P("dp", "tensor"),
        P(),
        P(None, "tensor"),
        P("tensor"),
        P(None, "tensor"),
        P("tensor"),
        P(None, "tensor"),
        P("tensor"),
        P("tensor", None, None),
        P("tensor"),
        P("tensor", None, None),
        P("tensor"),
        P("tensor"),
        P("tensor", None),
        P(),
        P(None, "tensor"),
        P(None, "tensor"),
        P("tensor", None),
    )
    return jax.shard_map(body, mesh=mesh, in_specs=in_specs, out_specs=out_specs, check_vma=False)
```

profile of v0, /device:TPU:0, one launch (start us, length us, event | category | flops | bytes accessed | tf_op | source)
XLA Modules:
  0.0 2209.8 jit_solution(8797544625298831027)
XLA Ops:
  21.3 19.5 all-gather.10.cloned.1.call-done
  319.4 118.9 %all-reduce.76.cloned.1.call-done = f32[1024,1536]{1,0:T(8,128)} async-done(((f32[1024,1536]{1,0:T(8,128)}), f32[1024,1536]{1,0:T(8,128)}) %all-reduce.76.cloned.1.call-update) | async-done | bytes 6291472 | tf_op jit(solution)/shard_map/psum | solution.py:133
  468.6 12.3 multiply_convert_fusion.2
  545.0 66.2 %all-reduce.78.cloned.1.call-done = f32[1024,1536]{1,0:T(8,128)} async-done(((f32[1024,1536]{1,0:T(8,128)}), f32[1024,1536]{1,0:T(8,128)}) %all-reduce.78.cloned.1.call-update) | async-done | bytes 6291472 | tf_op jit(solution)/shard_map/psum | solution.py:160
  874.5 16.6 rev.2
  1008.3 73.4 %reduce-scatter.23.cloned.1.call-done = f32[64,1536]{1,0:T(8,128)} async-done(((f32[512,1536]{1,0:T(8,128)}), f32[64,1536]{1,0:T(8,128)}) %reduce-scatter.23.cloned.1.call-update) | async-done | bytes 393232 | tf_op jit(solution)/shard_map/reduce_scatter | solution.py:213
  1083.5 75.9 %reduce-scatter.15.cloned.1.call-done = f32[192,512]{1,0:T(8,128)} async-done(((f32[1536,512]{1,0:T(8,128)}), f32[192,512]{1,0:T(8,128)}) %reduce-scatter.15.cloned.1.call-update) | async-done | bytes 393232 | tf_op jit(solution)/shard_map/reduce_scatter | solution.py:202
  1161.3 130.8 %reduce-scatter.25.cloned.1.call-done = f32[192,1152]{1,0:T(8,128)} async-done(((f32[1536,1152]{1,0:T(8,128)}), f32[192,1152]{1,0:T(8,128)}) %reduce-scatter.25.cloned.1.call-update) | async-done | bytes 884752 | tf_op jit(solution)/shard_map/reduce_scatter | solution.py:215
  1294.1 130.5 %reduce-scatter.27.cloned.1.call-done = f32[192,1152]{1,0:T(8,128)} async-done(((f32[1536,1152]{1,0:T(8,128)}), f32[192,1152]{1,0:T(8,128)}) %reduce-scatter.27.cloned.1.call-update) | async-done | bytes 884752 | tf_op jit(solution)/shard_map/reduce_scatter | solution.py:216
  1426.7 130.4 %reduce-scatter.29.cloned.1.call-done = f32[1152,192]{0,1:T(8,128)} async-done(((f32[1152,1536]{0,1:T(8,128)}), f32[1152,192]{0,1:T(8,128)}) %reduce-scatter.29.cloned.1.call-update) | async-done | bytes 884752 | tf_op jit(solution)/shard_map/reduce_scatter | solution.py:217
  1567.7 54.5 %reduce-scatter.33.cloned.1.call-done = f32[64,4]{1,0:T(8,128)} async-done(((f32[512,4]{1,0:T(8,128)}), f32[64,4]{1,0:T(8,128)}) %reduce-scatter.33.cloned.1.call-update) | async-done | bytes 1040
  1623.0 18.6 all-gather
  1642.3 45.2 %reduce-scatter.19.cloned.1.call-done = f32[4,16,128]{2,1,0:T(8,128)} async-done(((f32[4,128,128]{2,1,0:T(8,128)}), f32[4,16,128]{2,1,0:T(8,128)}) %reduce-scatter.19.cloned.1.call-update) | async-done | bytes 32784 | tf_op jit(solution)/shard_map/reduce_scatter | solution.py:208
  1688.3 30.6 %all_gather.66 = bf16[4,128,128]{2,1,0:T(8,128)(2,1)S(1)} all-gather(bf16[4,16,128]{2,1,0:T(8,128)(2,1)S(1)} %convert_element_type.250), channel_id=1, replica_groups=mesh['dp'=8,'tensor'=4] {'dp'}, dimensions={1}, use_global_device_ids=true | all-gather | bytes 147456 | tf_op jit(solution)/shard_map/all_gather | solution.py:241
  1719.6 33.4 %reduce-scatter.21.cloned.1.call-done = f32[4,16,128]{2,1,0:T(8,128)} async-done(((f32[4,128,128]{2,1,0:T(8,128)}), f32[4,16,128]{2,1,0:T(8,128)}) %reduce-scatter.21.cloned.1.call-update) | async-done | bytes 32784 | tf_op jit(solution)/shard_map/reduce_scatter | solution.py:210
  1753.7 30.8 %all_gather.68 = bf16[4,128,128]{2,1,0:T(8,128)(2,1)S(1)} all-gather(bf16[4,16,128]{2,1,0:T(8,128)(2,1)S(1)} %convert_element_type.255), channel_id=1, replica_groups=mesh['dp'=8,'tensor'=4] {'dp'}, dimensions={1}, use_global_device_ids=true | all-gather | bytes 147456 | tf_op jit(solution)/shard_map/all_gather | solution.py:247
  1785.2 38.1 %all-reduce.80.cloned.1.call-done = bf16[1024,1536]{1,0:T(8,128)(2,1)} async-done(((bf16[1024,1536]{1,0:T(8,128)(2,1)}), bf16[1024,1536]{1,0:T(8,128)(2,1)}) %all-reduce.80.cloned.1.call-update) | async-done | bytes 3145744 | tf_op jit(solution)/shard_map/psum | solution.py:197
  1830.2 38.4 %all-reduce.70 = (bf16[1536]{0:T(1024)(128)(2,1)}, bf16[512]{0:T(512)(128)(2,1)}, bf16[512]{0:T(512)(128)(2,1)}, bf16[512]{0:T(512)(128)(2,1)}, bf16[512]{0:T(51...) all-reduce(f32[1536]{0:T(1024)} %get-tuple-element.116, ...), channel_id=3, replica_groups=mesh['dp'=8,'tensor'=4] {'dp'}, use_global_device_ids=true, to_apply=%region_9.10.clone | all-reduce | flops 6144 | bytes 36864
  1887.8 34.5 %all-reduce.71 = (bf16[1536]{0:T(1024)(128)(2,1)}, bf16[512]{0:T(512)(128)(2,1)}, bf16[512]{0:T(512)(128)(2,1)}, bf16[512]{0:T(512)(128)(2,1)}, bf16[512]{0:T(51...) all-reduce(bf16[1536]{0:T(1024)(128)(2,1)S(1)} %dynamic-update-slic, ...), channel_id=1, replica_groups=mesh['dp'=8,'tensor'=4] {'dp'}, use_global_device_ids=true, to_apply=%add.54 | all-reduce | flops 6144 | bytes 24576
  1945.6 10.5 all-gather.18.cloned.1.call-done
  1959.6 41.1 %all-gather.14.cloned.1.call-done = bf16[1536,512]{1,0:T(8,128)(2,1)} async-done(((bf16[192,512]{1,0:T(8,128)(2,1)}), bf16[1536,512]{1,0:T(8,128)(2,1)}) %all-gather.14.cloned.1.call-update) | async-done | bytes 1572880 | tf_op jit(solution)/shard_map/all_gather | solution.py:223
  2004.2 61.7 %all-gather.20.cloned.1.call-done = bf16[1536,1152]{1,0:T(8,128)(2,1)} async-done(((bf16[192,1152]{1,0:T(8,128)(2,1)}), bf16[1536,1152]{1,0:T(8,128)(2,1)}) %all-gather.20.cloned.1.call-update) | async-done | bytes 3538960 | tf_op jit(solution)/shard_map/all_gather | solution.py:262
  2071.3 60.0 %all-gather.22.cloned.1.call-done = bf16[1536,1152]{1,0:T(8,128)(2,1)} async-done(((bf16[192,1152]{1,0:T(8,128)(2,1)}), bf16[1536,1152]{1,0:T(8,128)(2,1)}) %all-gather.22.cloned.1.call-update) | async-done | bytes 3538960 | tf_op jit(solution)/shard_map/all_gather | solution.py:265
  2136.7 60.1 %all-gather.24.cloned.1.call-done = bf16[1152,1536]{0,1:T(8,128)(2,1)} async-done(((bf16[1152,192]{0,1:T(8,128)(2,1)}), bf16[1152,1536]{0,1:T(8,128)(2,1)}) %all-gather.24.cloned.1.call-update) | async-done | bytes 3538960 | tf_op jit(solution)/shard_map/all_gather | solution.py:268
  (565 shorter events, 860.0 us)
Async XLA Ops:
  7.2 461.4 %copy-start = (bf16[1152,1536]{1,0:T(8,128)(2,1)S(1)}, bf16[1152,1536]{1,0:T(8,128)(2,1)}, u32[]{:S(2)}) copy-start(bf16[1152,1536]{1,0:T(8,128)(2,1)} %param.39) | copy-start | bytes 10616836
  7.2 33.6 %all-gather.10.cloned.1.call-start = ((), (), s32[]{:S(2)}) async-start(), calls=%async_computation.10 | async-start | bytes 3932160 | tf_op jit(solution)/shard_map/all_gather | solution.py:105
  7.9 430.4 %all-reduce.76.cloned.1.call-start = ((), (), s32[]{:S(2)}) async-start(), calls=%async_computation.11 | async-start | bytes 12582912 | tf_op jit(solution)/shard_map/psum | solution.py:133
  318.6 150.0 %all-gather.12.cloned.1.call-start = ((), (), s32[]{:S(2)}) async-start(), calls=%async_computation.12 | async-start | bytes 3932160 | tf_op jit(solution)/shard_map/all_gather | solution.py:148
  319.3 291.9 %all-reduce.78.cloned.1.call-start = ((), (), s32[]{:S(2)}) async-start(), calls=%async_computation.13 | async-start | bytes 12582912 | tf_op jit(solution)/shard_map/psum | solution.py:160
  491.5 515.1 %reduce-scatter.17.cloned.1.call-start = ((), (), s32[]{:S(2)}) async-start(), calls=%async_computation.17 | async-start | bytes 3538944 | tf_op jit(solution)/shard_map/reduce_scatter | solution.py:204
  929.9 151.9 %reduce-scatter.23.cloned.1.call-start = ((), (), s32[]{:S(2)}) async-start(), calls=%async_computation.21 | async-start | bytes 3538944 | tf_op jit(solution)/shard_map/reduce_scatter | solution.py:213
  936.7 222.8 %reduce-scatter.15.cloned.1.call-start = ((), (), s32[]{:S(2)}) async-start(), calls=%async_computation.15 | async-start | bytes 3538944 | tf_op jit(solution)/shard_map/reduce_scatter | solution.py:202
  942.7 349.3 %reduce-scatter.25.cloned.1.call-start = ((), (), s32[]{:S(2)}) async-start(), calls=%async_computation.23 | async-start | bytes 7962624 | tf_op jit(solution)/shard_map/reduce_scatter | solution.py:215
  952.7 471.9 %reduce-scatter.27.cloned.1.call-start = ((), (), s32[]{:S(2)}) async-start(), calls=%async_computation.25 | async-start | bytes 7962624 | tf_op jit(solution)/shard_map/reduce_scatter | solution.py:216
  962.8 594.3 %reduce-scatter.29.cloned.1.call-start = ((), (), s32[]{:S(2)}) async-start(), calls=%async_computation.27 | async-start | bytes 7962624 | tf_op jit(solution)/shard_map/reduce_scatter | solution.py:217
  973.2 649.0 %reduce-scatter.33.cloned.1.call-start = ((), (), s32[]{:S(2)}) async-start(), calls=%async_computation.30 | async-start | bytes 294912
  975.4 712.1 %reduce-scatter.19.cloned.1.call-start = ((), (), s32[]{:S(2)}) async-start(), calls=%async_computation.19 | async-start | bytes 294912 | tf_op jit(solution)/shard_map/reduce_scatter | solution.py:208
  978.2 774.8 %reduce-scatter.21.cloned.1.call-start = ((), (), s32[]{:S(2)}) async-start(), calls=%async_computation.20 | async-start | bytes 294912 | tf_op jit(solution)/shard_map/reduce_scatter | solution.py:210
  987.1 836.3 %all-reduce.80.cloned.1.call-start = ((), (), s32[]{:S(2)}) async-start(), calls=%async_computation.14 | async-start | bytes 6291456 | tf_op jit(solution)/shard_map/psum | solution.py:197
  994.5 942.5 %reduce-scatter.31.cloned.1.call-start = ((), (), s32[]{:S(2)}) async-start(), calls=%async_computation.29 | async-start | bytes 3932160
  1006.5 935.6 %all-gather.16.cloned.1.call-start = ((), (), s32[]{:S(2)}) async-start(), calls=%async_computation.18 | async-start | bytes 1769472 | tf_op jit(solution)/shard_map/all_gather | solution.py:229
  1008.3 947.8 %all-gather.18.cloned.1.call-start = ((), (), s32[]{:S(2)}) async-start(), calls=%async_computation.22 | async-start | bytes 1769472 | tf_op jit(solution)/shard_map/all_gather | solution.py:256
  1083.5 917.2 %all-gather.14.cloned.1.call-start = ((), (), s32[]{:S(2)}) async-start(), calls=%async_computation.16 | async-start | bytes 1769472 | tf_op jit(solution)/shard_map/all_gather | solution.py:223
  1161.2 904.7 %all-gather.20.cloned.1.call-start = ((), (), s32[]{:S(2)}) async-start(), calls=%async_computation.24 | async-start | bytes 3981312 | tf_op jit(solution)/shard_map/all_gather | solution.py:262
  1294.1 265.0 %copy-start.63 = (u32[32]{0:T(128)S(1)}, u32[32]{0:T(128)}, u32[]{:S(2)}) copy-start(u32[32]{0:T(128)} %constant.193) | copy-start | bytes 388
  1294.1 837.2 %all-gather.22.cloned.1.call-start = ((), (), s32[]{:S(2)}) async-start(), calls=%async_computation.26 | async-start | bytes 3981312 | tf_op jit(solution)/shard_map/all_gather | solution.py:265
  1426.6 770.2 %all-gather.24.cloned.1.call-start = ((), (), s32[]{:S(2)}) async-start(), calls=%async_computation.28 | async-start | bytes 3981312 | tf_op jit(solution)/shard_map/all_gather | solution.py:268
  1785.2 147.9 %copy-start.26 = (f32[1024]{0:T(1024)S(1)}, f32[1024]{0:T(1024)}, u32[]{:S(2)}) copy-start(f32[1024]{0:T(1024)} %copy-done.23) | copy-start | bytes 12292
  (77 other events, 751.1 us)
Sparse Core Ops, SparseCore 0:
  9.6 31.1 all-gather.9
  318.7 119.5 all-reduce.75
  439.9 28.6 all-gather.11
  491.6 119.5 all-reduce.77
  930.0 74.7 reduce-scatter.16
  1008.2 73.4 reduce-scatter.22
  1085.3 74.0 reduce-scatter.14
  1163.7 128.2 reduce-scatter.24
  1296.3 128.2 reduce-scatter.26
  1428.7 128.2 reduce-scatter.28
  1560.9 61.1 reduce-scatter.32
  1625.9 61.5 reduce-scatter.18
  1691.4 61.5 reduce-scatter.20
  1755.8 67.5 all-reduce.79
  1826.3 37.9 reduce-scatter.30
  1866.9 44.3 all-gather.15
  1913.4 42.6 all-gather.17
  1958.1 42.5 all-gather.13
  2002.9 62.9 all-gather.19
  2067.9 63.3 all-gather.21
  2133.5 63.3 all-gather.23
where the time goes:
time: 2230 us; the launch traced here: 2210 us
  waiting for transfers between devices  1160 us (52%)
  local copies, waits for them, and re-layouts  501 us (22%)
  other arithmetic  237 us (11%)
  blocking collectives  153 us (7%)
  matrix products  138 us (6%)
    slice x66, local copies, waits for them, and re-layouts, body(): lax.associative_scan(combine, (keep_next, d_state), reverse=True)[1]  185 us
    slice x60, local copies, waits for them, and re-layouts, body(): state = lax.associative_scan(combine, (keep, drive))[1]  131 us
    reduce_scatter x1, waiting for transfers between devices, body(): lax.psum_scatter(ffn_gate_grad, 'dp', scatter_dimension=0, tiled=True)  131 us
    reduce_scatter x1, waiting for transfers between devices, body(): lax.psum_scatter(ffn_up_grad, 'dp', scatter_dimension=0, tiled=True)  130 us
    reduce_scatter x1, waiting for transfers between devices, body(): lax.psum_scatter(ffn_down_grad, 'dp', scatter_dimension=1, tiled=True)  130 us
    psum x1, waiting for transfers between devices, body(): resid = whole_in + lax.psum(partial_value, 'tensor')  119 us
    reduce_scatter x1, waiting for transfers between devices, body(): lax.psum_scatter(gate_weight_grad, 'dp', scatter_dimension=0, tiled=True)  75.9 us
    reduce_scatter x1, waiting for transfers between devices, body(): lax.psum_scatter(out_weight_grad, 'dp', scatter_dimension=0, tiled=True)  73.4 us
  transfers between devices with their start and end apart: 21, of which 18 were waited for; matrix products, arithmetic and copies ran while one was open for 11% of the time, Pallas kernels for 0%

commit v1 on v0

--- a/solution.py
+++ b/solution.py
@@ -157,7 +157,9 @@
     d_two_part = jnp.einsum(
         "tf,df->td", d_hgate, ffn_gate, preferred_element_type=jnp.float32
     ) + jnp.einsum("tf,df->td", d_hup, ffn_up, preferred_element_type=jnp.float32)
-    d_two = lax.psum(d_two_part, "tensor")
+    d_two = d_two_part
+    for hop in (1, 2):
+        d_two = d_two + lax.ppermute(d_two, "tensor", [(dev, dev ^ hop) for dev in range(4)])
     d_resid_norm, second_gain_grad = second_pull(d_two)
     d_resid = whole_cot.astype(jnp.float32) + d_resid_norm
     d_resid_low = d_resid.astype(jnp.bfloat16)

time: 2230 us -> 1890 us (0.85)
  waiting for transfers between devices: 1160 us -> 813 us
    reduce_scatter x1, waiting for transfers between devices: 131 us -> 0.02 us  [body(): lax.psum_scatter(ffn_gate_grad, 'dp', scatter_dimension=0, tiled=True)]
    reduce_scatter x1, waiting for transfers between devices: 130 us -> 0.02 us  [body(): lax.psum_scatter(ffn_up_grad, 'dp', scatter_dimension=0, tiled=True)]
    reduce_scatter x1, waiting for transfers between devices: 130 us -> 0.02 us  [body(): lax.psum_scatter(ffn_down_grad, 'dp', scatter_dimension=1, tiled=True)]
    ppermute x0 -> x2, waiting for transfers between devices: none -> 89.2 us  [body(): lax.ppermute(d_two, 'tensor', [(dev, dev ^ hop) for dev in range(4)])]
    psum x1 -> x0, waiting for transfers between devices: 66.2 us -> none  [body(): d_two = lax.psum(d_two_part, 'tensor')]
    all_gather x1, waiting for transfers between devices: 61.7 us -> 0.01 us  [body(): lax.all_gather(pieces[14].astype(jnp.bfloat16), 'dp', axis=0, tiled=True)]
    all_gather x1, waiting for transfers between devices: 60 us -> 11.9 us  [body(): lax.all_gather(pieces[15].astype(jnp.bfloat16), 'dp', axis=0, tiled=True)]
    all_gather x1, waiting for transfers between devices: 0.01 us -> 39 us  [body(): lax.all_gather(pieces[3].astype(jnp.bfloat16), 'dp', axis=0, tiled=True)]
  transfers between devices with their start and end apart: 21 -> 22, of which waited for: 18 -> 18; matrix products, arithmetic and copies ran while one was open for 11% -> 30% of each run, Pallas kernels for 0% -> 0%
where the time goes in v1:
time: 1890 us; the launch traced here: 1870 us
  waiting for transfers between devices  813 us (43%)
  local copies, waits for them, and re-layouts  501 us (27%)
  other arithmetic  246 us (13%)
  blocking collectives  155 us (8%)
  matrix products  132 us (7%)
    slice x66, local copies, waits for them, and re-layouts, body(): lax.associative_scan(combine, (keep_next, d_state), reverse=True)[1]  185 us
    slice x60, local copies, waits for them, and re-layouts, body(): state = lax.associative_scan(combine, (keep, drive))[1]  131 us
    psum x1, waiting for transfers between devices, body(): resid = whole_in + lax.psum(partial_value, 'tensor')  119 us
    unnamed x22, waiting for transfers between devices  92.2 us
    ppermute x2, waiting for transfers between devices, body(): lax.ppermute(d_two, 'tensor', [(dev, dev ^ hop) for dev in range(4)])  89.2 us
    reduce_scatter x1, waiting for transfers between devices, body(): lax.psum_scatter(gate_weight_grad, 'dp', scatter_dimension=0, tiled=True)  75.9 us
    reduce_scatter x1, waiting for transfers between devices, body(): lax.psum_scatter(out_weight_grad, 'dp', scatter_dimension=0, tiled=True)  75.3 us
    unnamed x2, blocking collectives  74.7 us
  transfers between devices with their start and end apart: 22, of which 18 were waited for; matrix products, arithmetic and copies ran while one was open for 30% of the time, Pallas kernels for 0%

profile of v1, /device:TPU:0, one launch (start us, length us, event | category | flops | bytes accessed | tf_op | source)
XLA Modules:
  0.0 1867.0 jit_solution(2670915282195766802)
XLA Ops:
  21.3 19.5 %all-gather.10.cloned.1.call-done = bf16[1024,1536]{1,0:T(8,128)(2,1)} async-done(((bf16[1024,384]{1,0:T(8,128)(2,1)}), bf16[1024,1536]{1,0:T(8,128)(2,1)}) %all-gather.10.cloned.1.call-update) | async-done | bytes 3145744 | tf_op jit(solution)/shard_map/all_gather | solution.py:105
  319.4 118.9 %all-reduce.75.cloned.1.call-done = f32[1024,1536]{1,0:T(8,128)} async-done(((f32[1024,1536]{1,0:T(8,128)}), f32[1024,1536]{1,0:T(8,128)}) %all-reduce.75.cloned.1.call-update) | async-done | bytes 6291472 | tf_op jit(solution)/shard_map/psum | solution.py:133
  468.6 12.6 multiply_convert_fusion.2
  511.2 9.9 collective-permute-done
  583.8 79.2 %collective-permute-done.1 = f32[1024,1536]{1,0:T(8,128)} collective-permute-done((f32[1024,1536]{1,0:T(8,128)}, f32[1024,1536]{1,0:T(8,128)}, u32[]{:S(2)}, u32[]{:S(2)}) %collective-permute-start.1) | collective-permute-done | bytes 6291488 | tf_op jit(solution)/shard_map/ppermute | solution.py:162
  931.7 16.6 rev.2
  1039.6 22.1 %reduce-scatter.17.cloned.1.call-done = f32[192,512]{1,0:T(8,128)} async-done(((f32[1536,512]{1,0:T(8,128)}), f32[192,512]{1,0:T(8,128)}) %reduce-scatter.17.cloned.1.call-update) | async-done | bytes 393232 | tf_op jit(solution)/shard_map/reduce_scatter | solution.py:206
  1063.4 75.3 %reduce-scatter.23.cloned.1.call-done = f32[64,1536]{1,0:T(8,128)} async-done(((f32[512,1536]{1,0:T(8,128)}), f32[64,1536]{1,0:T(8,128)}) %reduce-scatter.23.cloned.1.call-update) | async-done | bytes 393232 | tf_op jit(solution)/shard_map/reduce_scatter | solution.py:215
  1140.5 75.9 %reduce-scatter.15.cloned.1.call-done = f32[192,512]{1,0:T(8,128)} async-done(((f32[1536,512]{1,0:T(8,128)}), f32[192,512]{1,0:T(8,128)}) %reduce-scatter.15.cloned.1.call-update) | async-done | bytes 393232 | tf_op jit(solution)/shard_map/reduce_scatter | solution.py:204
  1227.0 29.4 %reduce-scatter.31.cloned.1.call-done = bf16[384,1024]{1,0:T(8,128)(2,1)} async-done(((bf16[1536,1024]{1,0:T(8,128)(2,1)}), bf16[384,1024]{1,0:T(8,128)(2,1)}) %reduce-scatter.31.cloned.1.call-update) | async-done | bytes 786448
  1261.4 61.1 %reduce-scatter.33.cloned.1.call-done = f32[64,4]{1,0:T(8,128)} async-done(((f32[512,4]{1,0:T(8,128)}), f32[64,4]{1,0:T(8,128)}) %reduce-scatter.33.cloned.1.call-update) | async-done | bytes 1040
  1323.3 18.6 all-gather
  1342.7 45.2 %reduce-scatter.19.cloned.1.call-done = f32[4,16,128]{2,1,0:T(8,128)} async-done(((f32[4,128,128]{2,1,0:T(8,128)}), f32[4,16,128]{2,1,0:T(8,128)}) %reduce-scatter.19.cloned.1.call-update) | async-done | bytes 32784 | tf_op jit(solution)/shard_map/reduce_scatter | solution.py:210
  1388.6 30.6 %all_gather.66 = bf16[4,128,128]{2,1,0:T(8,128)(2,1)S(1)} all-gather(bf16[4,16,128]{2,1,0:T(8,128)(2,1)S(1)} %convert_element_type.250), channel_id=1, replica_groups=mesh['dp'=8,'tensor'=4] {'dp'}, dimensions={1}, use_global_device_ids=true | all-gather | bytes 147456 | tf_op jit(solution)/shard_map/all_gather | solution.py:243
  1419.9 32.9 %reduce-scatter.21.cloned.1.call-done = f32[4,16,128]{2,1,0:T(8,128)} async-done(((f32[4,128,128]{2,1,0:T(8,128)}), f32[4,16,128]{2,1,0:T(8,128)}) %reduce-scatter.21.cloned.1.call-update) | async-done | bytes 32784 | tf_op jit(solution)/shard_map/reduce_scatter | solution.py:212
  1453.6 30.7 %all_gather.68 = bf16[4,128,128]{2,1,0:T(8,128)(2,1)S(1)} all-gather(bf16[4,16,128]{2,1,0:T(8,128)(2,1)S(1)} %convert_element_type.255), channel_id=1, replica_groups=mesh['dp'=8,'tensor'=4] {'dp'}, dimensions={1}, use_global_device_ids=true | all-gather | bytes 147456 | tf_op jit(solution)/shard_map/all_gather | solution.py:249
  1485.0 38.1 %all-reduce.77.cloned.1.call-done = bf16[1024,1536]{1,0:T(8,128)(2,1)} async-done(((bf16[1024,1536]{1,0:T(8,128)(2,1)}), bf16[1024,1536]{1,0:T(8,128)(2,1)}) %all-reduce.77.cloned.1.call-update) | async-done | bytes 3145744 | tf_op jit(solution)/shard_map/psum | solution.py:199
  1530.0 40.1 %all-reduce.70 = (bf16[1536]{0:T(1024)(128)(2,1)}, bf16[512]{0:T(512)(128)(2,1)}, bf16[512]{0:T(512)(128)(2,1)}, bf16[512]{0:T(512)(128)(2,1)}, bf16[512]{0:T(51...) all-reduce(f32[1536]{0:T(1024)} %get-tuple-element.116, ...), channel_id=3, replica_groups=mesh['dp'=8,'tensor'=4] {'dp'}, use_global_device_ids=true, to_apply=%region_8.9.clone | all-reduce | flops 6144 | bytes 36864
  1589.5 34.6 %all-reduce.71 = (bf16[1536]{0:T(1024)(128)(2,1)}, bf16[512]{0:T(512)(128)(2,1)}, bf16[512]{0:T(512)(128)(2,1)}, bf16[512]{0:T(512)(128)(2,1)}, bf16[512]{0:T(51...) all-reduce(bf16[1536]{0:T(1024)(128)(2,1)S(1)} %dynamic-update-slic, ...), channel_id=1, replica_groups=mesh['dp'=8,'tensor'=4] {'dp'}, use_global_device_ids=true, to_apply=%add.54 | all-reduce | flops 6144 | bytes 24576
  1644.2 11.9 all-gather.22.cloned.1.call-done
  1661.5 60.0 %all-gather.24.cloned.1.call-done = bf16[1152,1536]{0,1:T(8,128)(2,1)} async-done(((bf16[1152,192]{0,1:T(8,128)(2,1)}), bf16[1152,1536]{0,1:T(8,128)(2,1)}) %all-gather.24.cloned.1.call-update) | async-done | bytes 3538960 | tf_op jit(solution)/shard_map/all_gather | solution.py:270
  1727.5 39.0 %all-gather.16.cloned.1.call-done = bf16[1536,512]{1,0:T(8,128)(2,1)} async-done(((bf16[192,512]{1,0:T(8,128)(2,1)}), bf16[1536,512]{1,0:T(8,128)(2,1)}) %all-gather.16.cloned.1.call-update) | async-done | bytes 1572880 | tf_op jit(solution)/shard_map/all_gather | solution.py:231
  1770.0 41.2 %all-gather.18.cloned.1.call-done = bf16[512,1536]{1,0:T(8,128)(2,1)} async-done(((bf16[64,1536]{1,0:T(8,128)(2,1)}), bf16[512,1536]{1,0:T(8,128)(2,1)}) %all-gather.18.cloned.1.call-update) | async-done | bytes 1572880 | tf_op jit(solution)/shard_map/all_gather | solution.py:258
  1814.7 41.7 %all-gather.14.cloned.1.call-done = bf16[1536,512]{1,0:T(8,128)(2,1)} async-done(((bf16[192,512]{1,0:T(8,128)(2,1)}), bf16[1536,512]{1,0:T(8,128)(2,1)}) %all-gather.14.cloned.1.call-update) | async-done | bytes 1572880 | tf_op jit(solution)/shard_map/all_gather | solution.py:225
  (577 shorter events, 863.8 us)
Async XLA Ops:
  7.2 461.4 %copy-start = (bf16[1152,1536]{1,0:T(8,128)(2,1)S(1)}, bf16[1152,1536]{1,0:T(8,128)(2,1)}, u32[]{:S(2)}) copy-start(bf16[1152,1536]{1,0:T(8,128)(2,1)} %param.39) | copy-start | bytes 10616836
  7.2 33.6 %all-gather.10.cloned.1.call-start = ((), (), s32[]{:S(2)}) async-start(), calls=%async_computation.10 | async-start | bytes 3932160 | tf_op jit(solution)/shard_map/all_gather | solution.py:105
  7.9 430.4 %all-reduce.75.cloned.1.call-start = ((), (), s32[]{:S(2)}) async-start(), calls=%async_computation.11 | async-start | bytes 12582912 | tf_op jit(solution)/shard_map/psum | solution.py:133
  318.6 150.0 %all-gather.12.cloned.1.call-start = ((), (), s32[]{:S(2)}) async-start(), calls=%async_computation.12 | async-start | bytes 3932160 | tf_op jit(solution)/shard_map/all_gather | solution.py:148
  319.3 714.0 %reduce-scatter.25.cloned.1.call-start = ((), (), s32[]{:S(2)}) async-start(), calls=%async_computation.22 | async-start | bytes 7962624 | tf_op jit(solution)/shard_map/reduce_scatter | solution.py:217
  489.0 546.4 %reduce-scatter.27.cloned.1.call-start = ((), (), s32[]{:S(2)}) async-start(), calls=%async_computation.24 | async-start | bytes 7962624 | tf_op jit(solution)/shard_map/reduce_scatter | solution.py:218
  498.9 538.6 %reduce-scatter.29.cloned.1.call-start = ((), (), s32[]{:S(2)}) async-start(), calls=%async_computation.26 | async-start | bytes 7962624 | tf_op jit(solution)/shard_map/reduce_scatter | solution.py:219
  510.9 10.2 collective-permute-start
  525.1 138.0 %collective-permute-start.1 = (f32[1024,1536]{1,0:T(8,128)}, f32[1024,1536]{1,0:T(8,128)}, u32[]{:S(2)}, u32[]{:S(2)}) collective-permute-start(f32[1024,1536]{1,0:T(8,128)} %add.517), channel_id=1, source_target_pairs={{0,2},{1,3},{2,0},{3,1},{4,6},{5,7},{6,4},{7,5},{8,10},{9,11},{10,... | collective-permute-start | bytes 18874376 | tf_op jit(solution)/shard_map/ppermute | solution.py:162
  583.6 478.1 %reduce-scatter.17.cloned.1.call-start = ((), (), s32[]{:S(2)}) async-start(), calls=%async_computation.16 | async-start | bytes 3538944 | tf_op jit(solution)/shard_map/reduce_scatter | solution.py:206
  987.1 151.7 %reduce-scatter.23.cloned.1.call-start = ((), (), s32[]{:S(2)}) async-start(), calls=%async_computation.20 | async-start | bytes 3538944 | tf_op jit(solution)/shard_map/reduce_scatter | solution.py:215
  994.2 222.2 %reduce-scatter.15.cloned.1.call-start = ((), (), s32[]{:S(2)}) async-start(), calls=%async_computation.14 | async-start | bytes 3538944 | tf_op jit(solution)/shard_map/reduce_scatter | solution.py:204
  1000.1 256.3 %reduce-scatter.31.cloned.1.call-start = ((), (), s32[]{:S(2)}) async-start(), calls=%async_computation.28 | async-start | bytes 3932160
  1012.2 310.3 %reduce-scatter.33.cloned.1.call-start = ((), (), s32[]{:S(2)}) async-start(), calls=%async_computation.29 | async-start | bytes 294912
  1014.4 373.5 %reduce-scatter.19.cloned.1.call-start = ((), (), s32[]{:S(2)}) async-start(), calls=%async_computation.18 | async-start | bytes 294912 | tf_op jit(solution)/shard_map/reduce_scatter | solution.py:210
  1017.2 435.6 %reduce-scatter.21.cloned.1.call-start = ((), (), s32[]{:S(2)}) async-start(), calls=%async_computation.19 | async-start | bytes 294912 | tf_op jit(solution)/shard_map/reduce_scatter | solution.py:212
  1026.1 497.0 %all-reduce.77.cloned.1.call-start = ((), (), s32[]{:S(2)}) async-start(), calls=%async_computation.13 | async-start | bytes 6291456 | tf_op jit(solution)/shard_map/psum | solution.py:199
  1033.3 605.5 %all-gather.20.cloned.1.call-start = ((), (), s32[]{:S(2)}) async-start(), calls=%async_computation.23 | async-start | bytes 3981312 | tf_op jit(solution)/shard_map/all_gather | solution.py:264
  1035.4 620.8 %all-gather.22.cloned.1.call-start = ((), (), s32[]{:S(2)}) async-start(), calls=%async_computation.25 | async-start | bytes 3981312 | tf_op jit(solution)/shard_map/all_gather | solution.py:267
  1037.5 180.7 %copy-start.68 = (u32[32]{0:T(128)S(1)}, u32[32]{0:T(128)}, u32[]{:S(2)}) copy-start(u32[32]{0:T(128)} %constant.193) | copy-start | bytes 388
  1037.5 684.0 %all-gather.24.cloned.1.call-start = ((), (), s32[]{:S(2)}) async-start(), calls=%async_computation.27 | async-start | bytes 3981312 | tf_op jit(solution)/shard_map/all_gather | solution.py:270
  1039.6 726.9 %all-gather.16.cloned.1.call-start = ((), (), s32[]{:S(2)}) async-start(), calls=%async_computation.17 | async-start | bytes 1769472 | tf_op jit(solution)/shard_map/all_gather | solution.py:231
  1063.4 747.8 %all-gather.18.cloned.1.call-start = ((), (), s32[]{:S(2)}) async-start(), calls=%async_computation.21 | async-start | bytes 1769472 | tf_op jit(solution)/shard_map/all_gather | solution.py:258
  1140.5 716.0 %all-gather.14.cloned.1.call-start = ((), (), s32[]{:S(2)}) async-start(), calls=%async_computation.15 | async-start | bytes 1769472 | tf_op jit(solution)/shard_map/all_gather | solution.py:225
  (83 other events, 961.4 us)
Sparse Core Ops, SparseCore 0:
  9.6 31.1 all-gather.9
  318.7 119.5 all-reduce.74
  439.9 28.6 all-gather.11
  489.1 129.1 reduce-scatter.24
  622.4 128.2 reduce-scatter.26
  754.8 128.2 reduce-scatter.28
  987.2 74.4 reduce-scatter.16
  1065.3 73.4 reduce-scatter.22
  1142.9 73.4 reduce-scatter.14
  1219.4 37.0 reduce-scatter.30
  1260.3 62.1 reduce-scatter.32
  1326.3 61.5 reduce-scatter.18
  1391.2 61.5 reduce-scatter.20
  1455.6 67.4 all-reduce.76
  1525.2 65.2 all-gather.19
  1592.5 63.5 all-gather.21
  1658.1 63.3 all-gather.23
  1723.5 42.8 all-gather.15
  1768.7 42.5 all-gather.17
  1813.8 42.5 all-gather.13
